TPU v7x, 32 devices: a whole 2x2x4 slice. The times are simulated.
32 devices in a mesh: dp: 16 (over z, x, core), tensor: 2 (over y).
Axes of the slice: x: 2, y: 2, z: 4, core: 2. Of those that a mesh axis runs over, the one named last changes fastest.
Arguments:
- tokens: bfloat16 [16, 512, 2048], P('dp', 'tensor'), may hold values from -6 to 6
- lengths: int32 [16], P('dp'), may hold values from 1 to 512, 5120 in all
- w_query: bfloat16 [2048, 256], P('dp', 'tensor'), may hold values from -0.125 to 0.125
- w_key: bfloat16 [2048, 256], P('dp', 'tensor'), may hold values from -0.125 to 0.125
- w_value: bfloat16 [2048, 2048], P('dp', 'tensor'), may hold values from -0.125 to 0.125
- w_output: bfloat16 [2048, 2048], P('tensor', 'dp'), may hold values from -2 to 2
- gain_one: bfloat16 [2048], P('dp'), may hold values from 0.099609375 to 1.8984375
- w_gate: bfloat16 [2048, 5632], P('dp', 'tensor'), may hold values from -0.125 to 0.125
- w_up: bfloat16 [2048, 5632], P('dp', 'tensor'), may hold values from -0.125 to 0.125
- w_down: bfloat16 [5632, 2048], P('tensor', 'dp'), may hold values from -0.078125 to 0.078125
- gain_two: bfloat16 [2048], P('dp'), may hold values from 0.099609375 to 1.8984375
- cotangent: bfloat16 [16, 512, 2048], P('dp', 'tensor'), may hold values from -6 to 6
Outputs:
- outputs: bfloat16 [16, 512, 2048], P('dp', 'tensor')
- input_grad: bfloat16 [16, 512, 2048], P('dp', 'tensor')
- grad_w_query: float32 [2048, 256], P('dp', 'tensor')
- grad_w_key: float32 [2048, 256], P('dp', 'tensor')
- grad_w_value: float32 [2048, 2048], P('dp', 'tensor')
- grad_w_output: float32 [2048, 2048], P('tensor', 'dp')
- grad_gain_one: float32 [2048], P('dp')
- grad_w_gate: float32 [2048, 5632], P('dp', 'tensor')
- grad_w_up: float32 [2048, 5632], P('dp', 'tensor')
- grad_w_down: float32 [5632, 2048], P('tensor', 'dp')
- grad_gain_two: float32 [2048], P('dp')
Inputs may be any that keep to these rules, and one draw needn't show every extreme that they name: `lengths`: the longest sequence fills all 512 slots.
All inputs are finite; a program needn't handle non-finite values. No bound on the sum of `lengths` on one device may be relied on, other than what follows from the above.
Results may differ from a plain program's by a relative error of at most 0.023.
Values may be sent and summed in bfloat16 or wider, within the bound.
No kernel may reach another device: no remote copies, remote signals or barrier semaphores. Data moves between devices by JAX's collectives and lax.ppermute only.
A program may use at most 192 MiB of HBM per device.

v0:
```python
import jax
import jax.numpy as jnp
from jax import lax
from jax.sharding import PartitionSpec as P

FD = 16
HV = 128
CH = 256


epsilon = 1e-05
top_precision = lax.Precision.HIGHEST


def rms_scale(value_rows):
    return lax.rsqrt(jnp.mean(value_rows * value_rows, axis=-1, keepdims=True) + epsilon)


def normalize(value_rows, gain_vec):
    return value_rows * rms_scale(value_rows) * gain_vec


def feature_map(vectors):
    feat_width = vectors.shape[-1]
    outer_prod = (vectors[..., :, None] * vectors[..., None, :]).reshape(
        vectors.shape[:-1] + (feat_width * feat_width,)
    )
    ones_col = jnp.ones(vectors.shape[:-1] + (1,), jnp.float32)
    return jnp.concatenate(
        [ones_col, vectors * feat_width ** (-0.25), outer_prod * (0.5 / feat_width) ** 0.5], axis=-1
    )


def block_step(carried, block_in):
    running_state, normal = carried
    queries, keys_in, value_rows = block_in
    feat_width = queries.shape[-1]
    scores = jnp.einsum("hqf,hkf->hqk", queries, keys_in, precision=top_precision) * feat_width ** (
        -0.5
    )
    row_index = lax.broadcasted_iota(jnp.int32, scores.shape, 1)
    col_index = lax.broadcasted_iota(jnp.int32, scores.shape, 2)
    layer_routine = jnp.where(row_index >= col_index, 1.0 + scores + 0.5 * scores * scores, 0.0)
    query_taylor_map = feature_map(queries)
    key_taylor_map = feature_map(keys_in)
    attention_numer = jnp.einsum(
        "atn,anx->atx", layer_routine, value_rows, precision=top_precision
    ) + jnp.einsum("pxo,poi->pxi", query_taylor_map, running_state, precision=top_precision)
    denominator = jnp.sum(layer_routine, axis=-1) + jnp.einsum(
        "hqf,hf->hq", query_taylor_map, normal, precision=top_precision
    )
    outputs = attention_numer / denominator[..., None]
    updated_state = running_state + jnp.einsum(
        "alb,alx->abx", key_taylor_map, value_rows, precision=top_precision
    )
    next_normal = normal + jnp.sum(key_taylor_map, axis=1)
    return ((updated_state, next_normal), outputs)


def attend(queries, keys_in, value_rows, head_count, block_len, key_width, value_width):
    row_total = queries.shape[0]
    blocks = row_total // block_len
    feat_count = 1 + key_width + key_width * key_width

    def to_blocks(flat_array, last_width):
        return flat_array.reshape(blocks, block_len, head_count, last_width).transpose(0, 2, 1, 3)

    initial = (
        jnp.zeros((head_count, feat_count, value_width), jnp.float32),
        jnp.zeros((head_count, feat_count), jnp.float32),
    )
    final_carry, outputs = lax.scan(
        jax.checkpoint(block_step),
        initial,
        (
            to_blocks(queries, key_width),
            to_blocks(keys_in, key_width),
            to_blocks(value_rows, value_width),
        ),
    )
    return outputs.transpose(0, 2, 1, 3).reshape(row_total, head_count * value_width)


def gather_attention(w_query, w_key, w_value, w_output, gain_one):
    return (
        lax.all_gather(w_query, "dp", axis=0, tiled=True),
        lax.all_gather(w_key, "dp", axis=0, tiled=True),
        lax.all_gather(w_value, "dp", axis=0, tiled=True),
        lax.all_gather(w_output, "dp", axis=1, tiled=True),
        lax.all_gather(gain_one, "dp", axis=0, tiled=True),
    )


def gather_feed(w_gate, w_up, w_down, gain_two):
    return (
        lax.all_gather(w_gate, "dp", axis=0, tiled=True),
        lax.all_gather(w_up, "dp", axis=0, tiled=True),
        lax.all_gather(w_down, "dp", axis=1, tiled=True),
        lax.all_gather(gain_two, "dp", axis=0, tiled=True),
    )


def spread(row_block):
    return lax.all_gather(row_block, "tensor", axis=0, tiled=True)


def collect(partial_terms):
    return lax.psum_scatter(
        partial_terms.astype(jnp.bfloat16), "tensor", scatter_dimension=0, tiled=True
    ).astype(jnp.float32)


def project(left_side, right_side):
    return jnp.dot(left_side, right_side, preferred_element_type=jnp.float32)


def contract_rows(left_side, right_side):
    return jnp.einsum("sa,sb->ab", left_side, right_side, preferred_element_type=jnp.float32)


def project_back(left_side, right_side):
    return jnp.einsum("sb,ab->sa", left_side, right_side, preferred_element_type=jnp.float32)


def per_device(
    tokens,
    lengths,
    w_query,
    w_key,
    w_value,
    w_output,
    gain_one,
    w_gate,
    w_up,
    w_down,
    gain_two,
    cotangent,
):
    local_rows = tokens.shape[1]
    head_count = w_query.shape[1] // FD
    row_start = lax.axis_index("tensor") * local_rows
    local_pos = row_start + lax.iota(jnp.int32, local_rows)
    mask_col = (local_pos < lengths[0]).astype(jnp.float32)[:, None]
    masked = tokens[0].astype(jnp.float32) * mask_col
    query_all, key_all, value_all, output_all, gain_one_all = gather_attention(
        w_query, w_key, w_value, w_output, gain_one
    )
    normed = spread(normalize(masked, gain_one_all.astype(jnp.float32)).astype(jnp.bfloat16))
    queries = project(normed, query_all).astype(jnp.bfloat16)
    keys_in = project(normed, key_all).astype(jnp.bfloat16)
    value_rows = project(normed, value_all).astype(jnp.bfloat16)

    def local_attention(query_in, key_in, value_in):
        return attend(query_in, key_in, value_in, head_count, CH, FD, HV)

    mixed_exact, attend_back = jax.vjp(
        local_attention,
        queries.astype(jnp.float32),
        keys_in.astype(jnp.float32),
        value_rows.astype(jnp.float32),
    )
    mixed = mixed_exact.astype(jnp.bfloat16)
    hidden = masked + collect(project(mixed, output_all))
    gate_all, up_all, down_all, gain_two_all = gather_feed(w_gate, w_up, w_down, gain_two)
    normed_two = spread(normalize(hidden, gain_two_all.astype(jnp.float32)).astype(jnp.bfloat16))
    gate_val = project(normed_two, gate_all)
    upward = project(normed_two, up_all)
    sigmoid_gate = jax.nn.sigmoid(gate_val)
    silu_val = gate_val * sigmoid_gate
    activation = (silu_val * upward).astype(jnp.bfloat16)
    feed_out = collect(project(activation, down_all))
    result = ((hidden + feed_out) * mask_col).astype(jnp.bfloat16)[None]
    gate_all, up_all, down_all, gain_two_all = gather_feed(w_gate, w_up, w_down, gain_two)
    output_back = cotangent[0].astype(jnp.float32) * mask_col
    feed_back = spread(output_back.astype(jnp.bfloat16))
    grad_down = contract_rows(activation, feed_back)
    act_back = project_back(feed_back, down_all)
    upward_back = (act_back * silu_val).astype(jnp.bfloat16)
    gate_back = (act_back * upward * sigmoid_gate * (1.0 + gate_val * (1.0 - sigmoid_gate))).astype(
        jnp.bfloat16
    )
    grad_gate = contract_rows(normed_two, gate_back)
    grad_upward = contract_rows(normed_two, upward_back)
    normed_two_back = collect(project_back(gate_back, gate_all) + project_back(upward_back, up_all))
    norm_out, norm_two_pull = jax.vjp(normalize, hidden, gain_two_all.astype(jnp.float32))
    hidden_norm_back, gain_two_back = norm_two_pull(normed_two_back)
    hidden_back = output_back + hidden_norm_back
    query_all, key_all, value_all, output_all, gain_one_all = gather_attention(
        w_query, w_key, w_value, w_output, gain_one
    )
    branch_back = spread(hidden_back.astype(jnp.bfloat16))
    grad_output = contract_rows(mixed, branch_back)
    mixed_back = project_back(branch_back, output_all)
    query_back, key_back, value_back = attend_back(mixed_back)
    query_round = query_back.astype(jnp.bfloat16)
    key_round = key_back.astype(jnp.bfloat16)
    value_round = value_back.astype(jnp.bfloat16)
    grad_query = contract_rows(normed, query_round)
    grad_key = contract_rows(normed, key_round)
    grad_value = contract_rows(normed, value_round)
    normed_back = collect(
        project_back(query_round, query_all)
        + project_back(key_round, key_all)
        + project_back(value_round, value_all)
    )
    norm_one_out, norm_one_pull = jax.vjp(normalize, masked, gain_one_all.astype(jnp.float32))
    masked_back, gain_one_back = norm_one_pull(normed_back)
    input_grad = ((hidden_back + masked_back) * mask_col).astype(jnp.bfloat16)[None]
    summed = (
        lax.psum_scatter(grad_query, "dp", scatter_dimension=0, tiled=True),
        lax.psum_scatter(grad_key, "dp", scatter_dimension=0, tiled=True),
        lax.psum_scatter(grad_value, "dp", scatter_dimension=0, tiled=True),
        lax.psum_scatter(grad_output, "dp", scatter_dimension=1, tiled=True),
        lax.psum_scatter(gain_one_back, "dp", scatter_dimension=0, tiled=True),
        lax.psum_scatter(grad_gate, "dp", scatter_dimension=0, tiled=True),
        lax.psum_scatter(grad_upward, "dp", scatter_dimension=0, tiled=True),
        lax.psum_scatter(grad_down, "dp", scatter_dimension=1, tiled=True),
        lax.psum_scatter(gain_two_back, "dp", scatter_dimension=0, tiled=True),
    )
    attn_grads = summed[:5]
    feed_grads = summed[5:]
    gain_totals = lax.psum((attn_grads[4], feed_grads[3]), "tensor")
    return (
        result,
        input_grad,
        attn_grads[0],
        attn_grads[1],
        attn_grads[2],
        attn_grads[3],
        gain_totals[0],
        feed_grads[0],
        feed_grads[1],
        feed_grads[2],
        gain_totals[1],
    )


def solution(mesh):
    return jax.shard_map(
        per_device,
        mesh=mesh,
        in_specs=(
            P("dp", "tensor", None),
            P("dp"),
            P("dp", "tensor"),
            P("dp", "tensor"),
            P("dp", "tensor"),
            P("tensor", "dp"),
            P("dp"),
            P("dp", "tensor"),
            P("dp", "tensor"),
            P("tensor", "dp"),
            P("dp"),
            P("dp", "tensor", None),
        ),
        out_specs=(
            P("dp", "tensor", None),
            P("dp", "tensor", None),
            P("dp", "tensor"),
            P("dp", "tensor"),
            P("dp", "tensor"),
            P("tensor", "dp"),
            P("dp"),
            P("dp", "tensor"),
            P("dp", "tensor"),
            P("tensor", "dp"),
            P("dp"),
        ),
        check_vma=False,
    )
```

profile of v0, /device:TPU:0, one launch (start us, length us, event | category | flops | bytes accessed | tf_op | source)
XLA Modules:
  0.0 1917.0 jit_solution(5352220012986960125)
XLA Ops:
  10.1 23.1 %all-gather = bf16[16,1,128]{2,1,0:T(2,128)(2,1)S(1)} all-gather(bf16[1,1,128]{2,1,0:T(2,128)(2,1)} %bitcast.335), channel_id=1, replica_groups=mesh['dp'=16,'tensor'=2] {'dp'}, dimensions={0}, use_global_device_ids=true | all-gather | bytes 4352 | tf_op jit(solution)/shard_map/all_gather | solution.py:90
  37.9 20.2 %all_gather.50 = bf16[2048,128]{1,0:T(8,128)(2,1)} all-gather(bf16[128,128]{1,0:T(8,128)(2,1)S(1)} %copy-done.43), channel_id=1, replica_groups=mesh['dp'=16,'tensor'=2] {'dp'}, dimensions={0}, use_global_device_ids=true | all-gather | bytes 557056 | tf_op jit(solution)/shard_map/all_gather | solution.py:87
  58.2 21.8 %all_gather.52 = bf16[2048,128]{1,0:T(8,128)(2,1)} all-gather(bf16[128,128]{1,0:T(8,128)(2,1)S(1)} %copy-done.44), channel_id=1, replica_groups=mesh['dp'=16,'tensor'=2] {'dp'}, dimensions={0}, use_global_device_ids=true | all-gather | bytes 557056 | tf_op jit(solution)/shard_map/all_gather | solution.py:86
  92.9 26.9 %all-gather.14.cloned.1.call-done = bf16[2048,1024]{1,0:T(8,128)(2,1)} async-done(((bf16[128,1024]{1,0:T(8,128)(2,1)}), bf16[2048,1024]{1,0:T(8,128)(2,1)}) %all-gather.14.cloned.1.call-update) | async-done | bytes 4194320 | tf_op jit(solution)/shard_map/all_gather | solution.py:88
  127.8 41.5 %while.45 = (s32[]{:T(128)}, f32[8,273,128]{2,1,0:T(8,128)S(1)}, f32[8,273]{1,0:T(8,128)S(1)}, bf16[2,8,256,128]{3,2,1,0:T(8,128)(2,1)}, f32[2,8,273,128]{3,2,1,...) while((s32[]{:T(128)}, f32[8,273,128]{2,1,0:T(8,128)S(1)}, ...), condition=%wide.region_4.5_spmd.clone, body=%wide.region_1.4_spmd.clone.sunk | while | flops 2643282176 | bytes 65933104 | solution.py:72
  180.3 18.5 all-gather.1
  198.8 11.0 reduce-scatter.12.cloned.1.call-done
  216.4 30.4 %all-gather.18.cloned.1.call-done = bf16[512,2048]{1,0:T(8,128)(2,1)} async-done(((bf16[256,2048]{1,0:T(8,128)(2,1)}), bf16[512,2048]{1,0:T(8,128)(2,1)}) %all-gather.18.cloned.1.call-update) | async-done | bytes 2097168 | tf_op jit(solution)/shard_map/all_gather | solution.py:104
  246.9 96.7 %all-gather.20.cloned.1.call-done = bf16[2048,2816]{1,0:T(8,128)(2,1)} async-done(((bf16[128,2816]{1,0:T(8,128)(2,1)}), bf16[2048,2816]{1,0:T(8,128)(2,1)}) %all-gather.20.cloned.1.call-update) | async-done | bytes 11534352 | tf_op jit(solution)/shard_map/all_gather | solution.py:96
  343.6 12.5 fusion.113
  356.1 82.6 %all-gather.22.cloned.1.call-done = bf16[2048,2816]{1,0:T(8,128)(2,1)} async-done(((bf16[128,2816]{1,0:T(8,128)(2,1)}), bf16[2048,2816]{1,0:T(8,128)(2,1)}) %all-gather.22.cloned.1.call-update) | async-done | bytes 11534352 | tf_op jit(solution)/shard_map/all_gather | solution.py:97
  438.7 12.5 fusion.114
  451.2 21.0 %all-gather.26.cloned.1.call-done = bf16[512,2048]{1,0:T(8,128)(2,1)} async-done(((bf16[256,2048]{1,0:T(8,128)(2,1)}), bf16[512,2048]{1,0:T(8,128)(2,1)}) %all-gather.26.cloned.1.call-update) | async-done | bytes 2097168 | tf_op jit(solution)/shard_map/all_gather | solution.py:104
  472.2 99.8 %all-gather.24.cloned.1.call-done = bf16[2816,2048]{1,0:T(8,128)(2,1)} async-done(((bf16[2816,128]{1,0:T(8,128)(2,1)}), bf16[2816,2048]{1,0:T(8,128)(2,1)}) %all-gather.24.cloned.1.call-update) | async-done | bytes 11534352 | tf_op jit(solution)/shard_map/all_gather | solution.py:98
  572.0 16.1 multiply_convert_fusion
  588.0 10.9 fusion.115
  599.0 10.2 add_convert_fusion.1
  609.2 30.1 %reduce-scatter.16.cloned.1.call-done = bf16[256,2048]{1,0:T(8,128)(2,1)} async-done(((bf16[512,2048]{1,0:T(8,128)(2,1)}), bf16[256,2048]{1,0:T(8,128)(2,1)}) %reduce-scatter.16.cloned.1.call-update) | async-done | bytes 1048592 | tf_op jit(solution)/shard_map/reduce_scatter | solution.py:108
  644.4 33.2 %all-gather.28.cloned.1.call-done = bf16[512,2048]{1,0:T(8,128)(2,1)} async-done(((bf16[256,2048]{1,0:T(8,128)(2,1)}), bf16[512,2048]{1,0:T(8,128)(2,1)}) %all-gather.28.cloned.1.call-update) | async-done | bytes 2097168 | tf_op jit(solution)/shard_map/all_gather | solution.py:104
  690.4 112.0 %while.46 = (s32[]{:T(128)}, f32[8,273,128]{2,1,0:T(8,128)}, f32[8,273]{1,0:T(8,128)S(1)}, bf16[2,8,256,16]{2,3,1,0:T(8,128)(2,1)}, bf16[2,8,256,16]{2,3,1,0:T(8...) while((s32[]{:T(128)}, f32[8,273,128]{2,1,0:T(8,128)}, ...), condition=%wide.region_17.18_spmd.clone, body=%wide.region_10.17_spmd.clone.sunk | while | flops 7061327872 | bytes 111617664 | solution.py:72
  811.6 10.8 convolution_convert_fusion.1
  827.6 7.3 fusion.101
  843.5 13.0 fusion.119
  856.6 12.8 fusion.120
  871.0 12.9 fusion.121
  887.9 61.3 %all-reduce.2 = (f32[2048]{0:T(1024)S(1)}, f32[2048]{0:T(1024)S(1)}) all-reduce(f32[2048]{0:T(1024)S(1)} %get-tuple-element.553, f32[2048]{0:T(1024)S(1)} %copy-done.42), channel_id=10, replica_groups=mesh['dp'=16,'tensor'=2] {'dp'}, use_global_device_ids=true, to_apply=%region_25.26.clone | all-reduce | flops 4096 | bytes 32768
  959.3 40.9 %reduce-scatter.22.cloned.1.call-done = f32[128,128]{1,0:T(8,128)} async-done(((f32[2048,128]{1,0:T(8,128)}), f32[128,128]{1,0:T(8,128)}) %reduce-scatter.22.cloned.1.call-update) | async-done | bytes 65552 | tf_op jit(solution)/shard_map/reduce_scatter | solution.py:211
  1000.2 108.4 %reduce-scatter.26.cloned.1.call-done = f32[1024,128]{1,0:T(8,128)} async-done(((f32[1024,2048]{1,0:T(8,128)}), f32[1024,128]{1,0:T(8,128)}) %reduce-scatter.26.cloned.1.call-update) | async-done | bytes 524304 | tf_op jit(solution)/shard_map/reduce_scatter | solution.py:213
  1108.6 108.9 %reduce-scatter.24.cloned.1.call-done = f32[128,1024]{1,0:T(8,128)} async-done(((f32[2048,1024]{1,0:T(8,128)}), f32[128,1024]{1,0:T(8,128)}) %reduce-scatter.24.cloned.1.call-update) | async-done | bytes 524304 | tf_op jit(solution)/shard_map/reduce_scatter | solution.py:212
  1217.5 231.2 %reduce-scatter.28.cloned.1.call-done = f32[128,2816]{1,0:T(8,128)} async-done(((f32[2048,2816]{1,0:T(8,128)}), f32[128,2816]{1,0:T(8,128)}) %reduce-scatter.28.cloned.1.call-update) | async-done | bytes 1441808 | tf_op jit(solution)/shard_map/reduce_scatter | solution.py:215
  1448.7 230.7 %reduce-scatter.30.cloned.1.call-done = f32[128,2816]{1,0:T(8,128)} async-done(((f32[2048,2816]{1,0:T(8,128)}), f32[128,2816]{1,0:T(8,128)}) %reduce-scatter.30.cloned.1.call-update) | async-done | bytes 1441808 | tf_op jit(solution)/shard_map/reduce_scatter | solution.py:216
  1679.4 230.5 %reduce-scatter.32.cloned.1.call-done = f32[2816,128]{1,0:T(8,128)} async-done(((f32[2816,2048]{1,0:T(8,128)}), f32[2816,128]{1,0:T(8,128)}) %reduce-scatter.32.cloned.1.call-update) | async-done | bytes 1441808 | tf_op jit(solution)/shard_map/reduce_scatter | solution.py:217
  (343 shorter events, 223.8 us)
Async XLA Ops:
  7.2 72.8 %all-gather.12.cloned.1.call-start = ((), (), s32[]{:S(2)}) async-start(), calls=%async_computation.11 | async-start | bytes 3145728 | tf_op jit(solution)/shard_map/all_gather | solution.py:104
  7.9 634.4 %copy-start.40 = (f32[256]{0:T(256)}, f32[256]{0:T(256)S(1)}, u32[]{:S(2)}) copy-start(f32[256]{0:T(256)S(1)} %compare_convert_fusion) | copy-start | bytes 3076
  10.1 48.1 %copy-start.47 = (f32[256]{0:T(256)}, f32[256]{0:T(256)S(1)}, u32[]{:S(2)}) copy-start(f32[256]{0:T(256)S(1)} %fusion.108) | copy-start | bytes 3076
  36.4 83.5 %all-gather.14.cloned.1.call-start = ((), (), s32[]{:S(2)}) async-start(), calls=%async_computation.12 | async-start | bytes 4456448 | tf_op jit(solution)/shard_map/all_gather | solution.py:88
  37.2 136.6 %all-gather.16.cloned.1.call-start = ((), (), s32[]{:S(2)}) async-start(), calls=%async_computation.13 | async-start | bytes 4456448 | tf_op jit(solution)/shard_map/all_gather | solution.py:89
  37.9 171.9 %reduce-scatter.12.cloned.1.call-start = ((), (), s32[]{:S(2)}) async-start(), calls=%async_computation.14 | async-start | bytes 3145728 | tf_op jit(solution)/shard_map/reduce_scatter | solution.py:108
  179.6 30.2 %copy-start.6 = (bf16[1,256,2048]{2,1,0:T(8,128)(2,1)S(1)}, bf16[1,256,2048]{2,1,0:T(8,128)(2,1)}, u32[]{:S(2)}) copy-start(bf16[1,256,2048]{2,1,0:T(8,128)(2,1)} %param.16) | copy-start | bytes 3145732
  179.6 32.1 %copy-start.15 = (bf16[1,256,2048]{2,1,0:T(8,128)(2,1)S(1)}, bf16[1,256,2048]{2,1,0:T(8,128)(2,1)}, u32[]{:S(2)}) copy-start(bf16[1,256,2048]{2,1,0:T(8,128)(2,1)} %param.27) | copy-start | bytes 3145732
  179.7 67.2 %all-gather.18.cloned.1.call-start = ((), (), s32[]{:S(2)}) async-start(), calls=%async_computation.15 | async-start | bytes 3145728 | tf_op jit(solution)/shard_map/all_gather | solution.py:104
  198.8 443.4 %copy-start.35 = (f32[16,1,128]{2,1,0:T(1,128)}, f32[16,1,128]{2,1,0:T(1,128)S(1)}, u32[]{:S(2)}) copy-start(f32[16,1,128]{2,1,0:T(1,128)S(1)} %convert_element_type.168) | copy-start | bytes 24580
  211.7 430.6 %copy-start.45 = (f32[256]{0:T(256)}, f32[256]{0:T(256)S(1)}, u32[]{:S(2)}) copy-start(f32[256]{0:T(256)S(1)} %fusion.109) | copy-start | bytes 3076
  213.6 130.0 %all-gather.20.cloned.1.call-start = ((), (), s32[]{:S(2)}) async-start(), calls=%async_computation.16 | async-start | bytes 12255232 | tf_op jit(solution)/shard_map/all_gather | solution.py:96
  214.2 224.5 %all-gather.22.cloned.1.call-start = ((), (), s32[]{:S(2)}) async-start(), calls=%async_computation.17 | async-start | bytes 12255232 | tf_op jit(solution)/shard_map/all_gather | solution.py:97
  214.9 257.3 %all-gather.26.cloned.1.call-start = ((), (), s32[]{:S(2)}) async-start(), calls=%async_computation.20 | async-start | bytes 3145728 | tf_op jit(solution)/shard_map/all_gather | solution.py:104
  215.7 356.3 %all-gather.24.cloned.1.call-start = ((), (), s32[]{:S(2)}) async-start(), calls=%async_computation.18 | async-start | bytes 12255232 | tf_op jit(solution)/shard_map/all_gather | solution.py:98
  216.4 423.0 %reduce-scatter.16.cloned.1.call-start = ((), (), s32[]{:S(2)}) async-start(), calls=%async_computation.21 | async-start | bytes 3145728 | tf_op jit(solution)/shard_map/reduce_scatter | solution.py:108
  609.2 68.5 %all-gather.28.cloned.1.call-start = ((), (), s32[]{:S(2)}) async-start(), calls=%async_computation.22 | async-start | bytes 3145728 | tf_op jit(solution)/shard_map/all_gather | solution.py:104
  644.4 241.4 %reduce-scatter.18.cloned.1.call-start = ((), (), s32[]{:S(2)}) async-start(), calls=%async_computation.23 | async-start | bytes 3145728 | tf_op jit(solution)/shard_map/reduce_scatter | solution.py:108
  811.6 143.3 %reduce-scatter.14.cloned.1.call-start = ((), (), s32[]{:S(2)}) async-start(), calls=%async_computation.19 | async-start | bytes 3145728 | tf_op jit(solution)/shard_map/reduce_scatter | solution.py:108
  822.5 136.9 %reduce-scatter.20.cloned.1.call-start = ((), (), s32[]{:S(2)}) async-start(), calls=%async_computation.24 | async-start | bytes 1114112 | tf_op jit(solution)/shard_map/reduce_scatter | solution.py:210
  825.8 174.4 %reduce-scatter.22.cloned.1.call-start = ((), (), s32[]{:S(2)}) async-start(), calls=%async_computation.25 | async-start | bytes 1114112 | tf_op jit(solution)/shard_map/reduce_scatter | solution.py:211
  827.6 281.0 %reduce-scatter.26.cloned.1.call-start = ((), (), s32[]{:S(2)}) async-start(), calls=%async_computation.27 | async-start | bytes 8912896 | tf_op jit(solution)/shard_map/reduce_scatter | solution.py:213
  835.0 382.6 %reduce-scatter.24.cloned.1.call-start = ((), (), s32[]{:S(2)}) async-start(), calls=%async_computation.26 | async-start | bytes 8912896 | tf_op jit(solution)/shard_map/reduce_scatter | solution.py:212
  842.0 606.8 %reduce-scatter.28.cloned.1.call-start = ((), (), s32[]{:S(2)}) async-start(), calls=%async_computation.28 | async-start | bytes 24510464 | tf_op jit(solution)/shard_map/reduce_scatter | solution.py:215
  856.6 822.8 %reduce-scatter.30.cloned.1.call-start = ((), (), s32[]{:S(2)}) async-start(), calls=%async_computation.29 | async-start | bytes 24510464 | tf_op jit(solution)/shard_map/reduce_scatter | solution.py:216
  869.4 1040.5 %reduce-scatter.32.cloned.1.call-start = ((), (), s32[]{:S(2)}) async-start(), calls=%async_computation.30 | async-start | bytes 24510464 | tf_op jit(solution)/shard_map/reduce_scatter | solution.py:217
  883.9 70.9 %copy-start.50 = (f32[256]{0:T(256)S(1)}, f32[256]{0:T(256)}, u32[]{:S(2)}) copy-start(f32[256]{0:T(256)} %copy-done.49) | copy-start | bytes 3076
  883.9 70.9 %copy-start.11 = (bf16[256,2048]{1,0:T(8,128)(2,1)S(1)}, bf16[256,2048]{1,0:T(8,128)(2,1)}, u32[]{:S(2)}) copy-start(bf16[256,2048]{1,0:T(8,128)(2,1)} %reduce-scatter.12.cloned.1.call-done) | copy-start | bytes 3145732
  883.9 70.9 %copy-start.16 = (bf16[1,256,2048]{2,1,0:T(8,128)(2,1)S(1)}, bf16[1,256,2048]{2,1,0:T(8,128)(2,1)}, u32[]{:S(2)}) copy-start(bf16[1,256,2048]{2,1,0:T(8,128)(2,1)} %param.27) | copy-start | bytes 3145732
  883.9 70.9 %copy-start.36 = (f32[16,1,128]{2,1,0:T(1,128)S(1)}, f32[16,1,128]{2,1,0:T(1,128)}, u32[]{:S(2)}) copy-start(f32[16,1,128]{2,1,0:T(1,128)} %copy-done.35) | copy-start | bytes 24580
  883.9 70.9 %copy-start.46 = (f32[256]{0:T(256)S(1)}, f32[256]{0:T(256)}, u32[]{:S(2)}) copy-start(f32[256]{0:T(256)} %copy-done.45) | copy-start | bytes 3076
  884.0 70.9 %copy-start.52 = (f32[256]{0:T(256)S(1)}, f32[256]{0:T(256)}, u32[]{:S(2)}) copy-start(f32[256]{0:T(256)} %copy-done.51) | copy-start | bytes 3076
  (64 other events, 209.8 us)
Sparse Core Ops, SparseCore 0:
  36.5 30.3 all-gather.11
  69.1 50.7 all-gather.13
  122.0 51.6 all-gather.15
  179.8 29.9 reduce-scatter.11
  213.7 33.1 all-gather.17
  249.3 94.3 all-gather.19
  346.1 92.4 all-gather.21
  440.9 31.2 all-gather.25
  474.6 97.3 all-gather.23
  609.3 30.0 reduce-scatter.15
  644.5 33.1 all-gather.27
  811.7 31.8 reduce-scatter.17
  845.9 31.8 reduce-scatter.13
  881.8 57.4 reduce-scatter.19
  943.7 56.4 reduce-scatter.21
  1004.7 103.8 reduce-scatter.25
  1113.1 104.3 reduce-scatter.23
  1222.1 226.6 reduce-scatter.27
  1453.4 225.9 reduce-scatter.29
  1683.9 225.9 reduce-scatter.31
where the time goes:
time: 1920 us
  waiting for transfers between devices  1390 us (72%)
  matrix products  251 us (13%)
  blocking collectives  150 us (8%)
  local copies, waits for them, and re-layouts  43.9 us (2%)
  other arithmetic  34.2 us (2%)
  loops' own time  30.6 us (2%)
    reduce_scatter x1, waiting for transfers between devices, per_device(): lax.psum_scatter(grad_gate, 'dp', scatter_dimension=0, tiled=True)  231 us
    reduce_scatter x1, waiting for transfers between devices, per_device(): lax.psum_scatter(grad_upward, 'dp', scatter_dimension=0, tiled=True)  231 us
    reduce_scatter x1, waiting for transfers between devices, per_device(): lax.psum_scatter(grad_down, 'dp', scatter_dimension=1, tiled=True)  231 us
    reduce_scatter x1, waiting for transfers between devices, per_device(): lax.psum_scatter(grad_value, 'dp', scatter_dimension=0, tiled=True)  109 us
    reduce_scatter x1, waiting for transfers between devices, per_device(): lax.psum_scatter(grad_output, 'dp', scatter_dimension=1, tiled=True)  108 us
    all_gather x1, waiting for transfers between devices, gather_feed(): lax.all_gather(w_down, 'dp', axis=1, tiled=True)  99.8 us
    all_gather x1, waiting for transfers between devices, gather_feed(): lax.all_gather(w_gate, 'dp', axis=0, tiled=True)  96.7 us
    all_gather x4, waiting for transfers between devices, spread(): return lax.all_gather(row_block, 'tensor', axis=0, tiled=True)  84.6 us
  transfers between devices with their start and end apart: 20, of which 16 were waited for; matrix products, arithmetic and copies ran while one was open for 8% of the time, Pallas kernels for 0%

commit v1 on v0

v1 whole, which is shorter than its diff:
```python
import jax
import jax.numpy as jnp
from jax import lax
from jax.experimental import pallas as pl
from jax.experimental.pallas import tpu as pltpu
from jax.sharding import Mesh, PartitionSpec as P

FD = 16
HV = 128
EPS = 1e-05
SWAP = [(0, 1), (1, 0)]
F32 = jnp.float32
BF16 = jnp.bfloat16


def dot(left, right, left_dim, right_dim):
    return lax.dot_general(
        left, right, (((left_dim,), (right_dim,)), ((), ())), preferred_element_type=F32
    )


def gather_rows(block):
    rows = block.shape[0]
    from_x = lax.ppermute(block, "x", SWAP)
    from_t = lax.ppermute(block, "t", SWAP)
    upper = lax.ppermute(from_t[: rows // 2], "x", SWAP)
    lower = lax.ppermute(from_x[rows // 2 :], "t", SWAP)
    near = jnp.concatenate([block, from_t, from_x, upper, lower], axis=0)
    far = lax.ppermute(near, "c", SWAP)
    return jnp.concatenate([near, far], axis=0)


def add(left, right):
    return (left.astype(F32) + right.astype(F32)).astype(BF16)


def scatter_rows(partial):
    total = partial.shape[0]
    here = add(partial[: total // 2], lax.ppermute(partial[total // 2 :], "c", SWAP))
    rows = total // 8
    half = rows // 2
    tops = [here[i * rows : i * rows + half] for i in range(4)]
    ends = [here[i * rows + half : (i + 1) * rows] for i in range(4)]
    got_x = lax.ppermute(jnp.concatenate([tops[2], tops[3]], axis=0), "x", SWAP)
    got_t = lax.ppermute(jnp.concatenate([ends[1], ends[3]], axis=0), "t", SWAP)
    last_t = lax.ppermute(add(tops[1], got_x[half:]), "t", SWAP)
    last_x = lax.ppermute(add(ends[2], got_t[half:]), "x", SWAP)
    top = tops[0].astype(F32) + got_x[:half].astype(F32) + last_t.astype(F32)
    end = ends[0].astype(F32) + got_t[:half].astype(F32) + last_x.astype(F32)
    return jnp.concatenate([top, end], axis=0)


def pick(array, axis, index):
    return lax.dynamic_index_in_dim(array, index, axis, keepdims=False)


def trade(array, split, join, axis_name):
    me = lax.axis_index(axis_name)
    kept = pick(array, split, me)
    got = lax.ppermute(pick(array, split, 1 - me), axis_name, SWAP)
    kept = jnp.expand_dims(kept, join)
    got = jnp.expand_dims(got, join)
    return jnp.where(
        me == 0,
        jnp.concatenate([kept, got], axis=join),
        jnp.concatenate([got, kept], axis=join),
    )


def inward_rows(weight):
    d, _, n = weight.shape
    step = trade(weight.reshape(d, 2, 2, n), 2, 0, "c")
    step = trade(step, 2, 0, "x")
    return step.reshape(4 * d, n)


def outward_rows(grad):
    d, n = grad.shape[0] // 4, grad.shape[1]
    step = trade(grad.reshape(2, 2, d, n), 0, 2, "x")
    step = trade(step, 0, 2, "c")
    return step.reshape(d, 4, n)


def inward_cols(weight):
    _, n, d = weight.shape
    step = trade(weight.reshape(2, 2, n, d), 1, 2, "c")
    step = trade(step, 0, 1, "x")
    return step.reshape(n, 4 * d)


def outward_cols(grad):
    n, d = grad.shape[0], grad.shape[1] // 4
    step = trade(grad.reshape(n, 2, 2, d), 1, 0, "x")
    step = trade(step, 2, 1, "c")
    return step.reshape(4, n, d)


def lanes_of(head, rows):
    lane = lax.broadcasted_iota(jnp.int32, (rows, 128), 1)
    return (lane >= head * FD) & (lane < (head + 1) * FD)


def head_parts(proj_ref, start, rows, heads):
    tile = proj_ref[pl.ds(start, rows), heads * HV :].astype(F32)
    keys = pltpu.roll(tile, 128 - heads * FD, 1)
    return tile, keys.astype(BF16)


def forward_kernel(half_ref, u_ref, w_ref, wo_ref, part_ref, proj_ref, mixed_ref, scale_ref):
    heads = wo_ref.shape[0] // HV
    size = u_ref.shape[0]
    rows = size // 2
    tokens = u_ref[...]
    wide = tokens.astype(F32)
    scale = lax.rsqrt(jnp.mean(wide * wide, axis=-1, keepdims=True) + EPS)
    scale_ref[...] = jnp.broadcast_to(scale, (size, 128))
    proj_ref[...] = (dot(tokens, w_ref[...], 1, 0) * scale).astype(BF16)
    first = pl.multiple_of(half_ref[0] * rows, rows)
    second = pl.multiple_of(rows - half_ref[0] * rows, rows)
    tile_a, keys_a = head_parts(proj_ref, first, rows, heads)
    tile_b, keys_b = head_parts(proj_ref, second, rows, heads)
    causal = lax.broadcasted_iota(jnp.int32, (rows, rows), 0) >= lax.broadcasted_iota(
        jnp.int32, (rows, rows), 1
    )

    def taylor(queries, keys):
        score = dot(queries, keys, 1, 1) * (FD**-0.5)
        return 1.0 + score + 0.5 * score * score

    for head in range(heads):
        here = lanes_of(head, rows)
        cols = slice(head * HV, (head + 1) * HV)
        query_a = jnp.where(here, tile_a, 0.0).astype(BF16)
        query_b = jnp.where(here, tile_b, 0.0).astype(BF16)
        value_a = proj_ref[pl.ds(first, rows), cols]
        value_b = proj_ref[pl.ds(second, rows), cols]
        aa = jnp.where(causal, taylor(query_a, keys_a), 0.0)
        bb = jnp.where(causal, taylor(query_b, keys_b), 0.0)
        ba = taylor(query_b, keys_a)
        den_a = jnp.sum(aa, axis=-1, keepdims=True)
        den_b = jnp.sum(bb, axis=-1, keepdims=True) + jnp.sum(ba, axis=-1, keepdims=True)
        out_a = dot(aa.astype(BF16), value_a, 1, 0) / den_a
        out_b = (dot(ba.astype(BF16), value_a, 1, 0) + dot(bb.astype(BF16), value_b, 1, 0)) / den_b
        mixed_ref[pl.ds(first, rows), cols] = out_a.astype(BF16)
        mixed_ref[pl.ds(second, rows), cols] = out_b.astype(BF16)
    part_ref[...] = dot(mixed_ref[...], wo_ref[...], 1, 0).astype(BF16)


def backward_kernel(
    half_ref, back_ref, u_ref, w_ref, wo_ref, proj_ref, mixed_ref, scale_ref,
    part_ref, grad_w_ref, grad_wo_ref, inner_ref, delta_ref, acc_w_ref, acc_wo_ref,
):
    heads = wo_ref.shape[0] // HV
    size = u_ref.shape[0]
    rows = size // 2
    step = pl.program_id(0)
    inner_ref[...] = dot(back_ref[...], wo_ref[...], 1, 1)
    first = pl.multiple_of(half_ref[0] * rows, rows)
    second = pl.multiple_of(rows - half_ref[0] * rows, rows)
    tile_a, keys_a = head_parts(proj_ref, first, rows, heads)
    tile_b, keys_b = head_parts(proj_ref, second, rows, heads)
    causal = lax.broadcasted_iota(jnp.int32, (rows, rows), 0) >= lax.broadcasted_iota(
        jnp.int32, (rows, rows), 1
    )
    scale_a = scale_ref[pl.ds(first, rows), :]
    scale_b = scale_ref[pl.ds(second, rows), :]
    zero = jnp.zeros((rows, 128), F32)
    query_back_a, query_back_b, key_back_a, key_back_b = zero, zero, zero, zero

    def score_of(queries, keys):
        return dot(queries, keys, 1, 1) * (FD**-0.5)

    for head in range(heads):
        here = lanes_of(head, rows)
        cols = slice(head * HV, (head + 1) * HV)
        query_a = jnp.where(here, tile_a, 0.0).astype(BF16)
        query_b = jnp.where(here, tile_b, 0.0).astype(BF16)
        value_a = proj_ref[pl.ds(first, rows), cols]
        value_b = proj_ref[pl.ds(second, rows), cols]
        s_aa, s_bb, s_ba = (
            score_of(query_a, keys_a),
            score_of(query_b, keys_b),
            score_of(query_b, keys_a),
        )
        k_aa = jnp.where(causal, 1.0 + s_aa + 0.5 * s_aa * s_aa, 0.0)
        k_bb = jnp.where(causal, 1.0 + s_bb + 0.5 * s_bb * s_bb, 0.0)
        k_ba = 1.0 + s_ba + 0.5 * s_ba * s_ba
        inv_a = 1.0 / jnp.sum(k_aa, axis=-1, keepdims=True)
        inv_b = 1.0 / (jnp.sum(k_bb, axis=-1, keepdims=True) + jnp.sum(k_ba, axis=-1, keepdims=True))
        g_a = inner_ref[pl.ds(first, rows), cols] * inv_a
        g_b = inner_ref[pl.ds(second, rows), cols] * inv_b
        c_a = -jnp.sum(g_a * mixed_ref[pl.ds(first, rows), cols].astype(F32), axis=-1, keepdims=True)
        c_b = -jnp.sum(g_b * mixed_ref[pl.ds(second, rows), cols].astype(F32), axis=-1, keepdims=True)
        g_a, g_b = g_a.astype(BF16), g_b.astype(BF16)
        value_back_a = dot(k_aa.astype(BF16), g_a, 0, 0) + dot(k_ba.astype(BF16), g_b, 0, 0)
        value_back_b = dot(k_bb.astype(BF16), g_b, 0, 0)
        delta_ref[pl.ds(first, rows), cols] = (value_back_a * scale_a).astype(BF16)
        delta_ref[pl.ds(second, rows), cols] = (value_back_b * scale_b).astype(BF16)
        d_aa = jnp.where(causal, (dot(g_a, value_a, 1, 1) + c_a) * (1.0 + s_aa), 0.0).astype(BF16)
        d_bb = jnp.where(causal, (dot(g_b, value_b, 1, 1) + c_b) * (1.0 + s_bb), 0.0).astype(BF16)
        d_ba = ((dot(g_b, value_a, 1, 1) + c_b) * (1.0 + s_ba)).astype(BF16)
        query_back_a += jnp.where(here, dot(d_aa, keys_a, 1, 0), 0.0)
        query_back_b += jnp.where(here, dot(d_bb, keys_b, 1, 0) + dot(d_ba, keys_a, 1, 0), 0.0)
        key_back_a += dot(d_aa, query_a, 0, 0) + dot(d_ba, query_b, 0, 0)
        key_back_b += dot(d_bb, query_b, 0, 0)
    shift = heads * FD
    tail = slice(heads * HV, heads * HV + 128)
    tile_back_a = (query_back_a + pltpu.roll(key_back_a, shift, 1)) * (scale_a * FD**-0.5)
    tile_back_b = (query_back_b + pltpu.roll(key_back_b, shift, 1)) * (scale_b * FD**-0.5)
    delta_ref[pl.ds(first, rows), tail] = tile_back_a.astype(BF16)
    delta_ref[pl.ds(second, rows), tail] = tile_back_b.astype(BF16)
    delta = delta_ref[...]
    part_ref[...] = dot(delta, w_ref[...], 1, 1).astype(BF16)

    @pl.when(step == 0)
    def _():
        acc_w_ref[...] = jnp.zeros_like(acc_w_ref)
        acc_wo_ref[...] = jnp.zeros_like(acc_wo_ref)

    acc_w_ref[...] += dot(u_ref[...], delta, 0, 0)
    acc_wo_ref[...] += dot(mixed_ref[...], back_ref[...], 0, 0)

    @pl.when(step == pl.num_programs(0) - 1)
    def _():
        grad_w_ref[...] = acc_w_ref[...].astype(BF16)
        grad_wo_ref[...] = acc_wo_ref[...].astype(BF16)


def attention(half, tokens, w_in, w_out, size):
    total, width = tokens.shape
    columns, inner = w_in.shape[1], w_out.shape[0]
    by_seq = lambda n: pl.BlockSpec((size, n), lambda i, half: (i, 0))
    whole = lambda a: pl.BlockSpec(a.shape, lambda i, half: (0, 0))
    return pl.pallas_call(
        forward_kernel,
        out_shape=(
            jax.ShapeDtypeStruct((total, width), BF16),
            jax.ShapeDtypeStruct((total, columns), BF16),
            jax.ShapeDtypeStruct((total, inner), BF16),
            jax.ShapeDtypeStruct((total, 128), F32),
        ),
        grid_spec=pltpu.PrefetchScalarGridSpec(
            num_scalar_prefetch=1,
            grid=(total // size,),
            in_specs=[by_seq(width), whole(w_in), whole(w_out)],
            out_specs=[by_seq(width), by_seq(columns), by_seq(inner), by_seq(128)],
        ),
        compiler_params=pltpu.CompilerParams(vmem_limit_bytes=40 << 20),
        cost_estimate=pl.CostEstimate(
            flops=2 * total * width * (columns + inner) + 8 * total * size * inner,
            bytes_accessed=4 * total * width + 4 * total * columns,
            transcendentals=total,
        ),
    )(half, tokens, w_in, w_out)


def attention_back(half, back, tokens, w_in, w_out, proj, mixed, scale, size):
    total, width = tokens.shape
    columns, inner = w_in.shape[1], w_out.shape[0]
    by_seq = lambda n: pl.BlockSpec((size, n), lambda i, half: (i, 0))
    whole = lambda a: pl.BlockSpec(a.shape, lambda i, half: (0, 0))
    return pl.pallas_call(
        backward_kernel,
        out_shape=(
            jax.ShapeDtypeStruct((total, width), BF16),
            jax.ShapeDtypeStruct(w_in.shape, BF16),
            jax.ShapeDtypeStruct(w_out.shape, BF16),
        ),
        grid_spec=pltpu.PrefetchScalarGridSpec(
            num_scalar_prefetch=1,
            grid=(total // size,),
            in_specs=[
                by_seq(width), by_seq(width), whole(w_in), whole(w_out),
                by_seq(columns), by_seq(inner), by_seq(128),
            ],
            out_specs=[by_seq(width), whole(w_in), whole(w_out)],
            scratch_shapes=[
                pltpu.VMEM((size, inner), F32),
                pltpu.VMEM((size, columns), BF16),
                pltpu.VMEM(w_in.shape, F32),
                pltpu.VMEM(w_out.shape, F32),
            ],
        ),
        compiler_params=pltpu.CompilerParams(vmem_limit_bytes=48 << 20),
        cost_estimate=pl.CostEstimate(
            flops=4 * total * width * (columns + inner) + 24 * total * size * inner,
            bytes_accessed=6 * total * width + 4 * total * columns,
            transcendentals=total,
        ),
    )(half, back, tokens, w_in, w_out, proj, mixed, scale)


def per_device(
    tokens, lengths, w_query, w_key, w_value, w_output, gain_one,
    w_gate, w_up, w_down, gain_two, cotangent,
):
    local_rows, width = tokens.shape[1:]
    shard = w_query.shape[0]
    heads = w_query.shape[1] // FD // 4
    hidden_units = w_gate.shape[1] // 4
    half = lax.axis_index("t")
    position = half * local_rows + lax.iota(jnp.int32, local_rows)
    mask = (position < lengths[0]).astype(F32)[:, None]
    half_index = jnp.reshape(half, (1,)).astype(jnp.int32)

    scale_one = gain_one.astype(F32)[:, None, None]
    parts = jnp.concatenate(
        [
            w_value.reshape(shard, 4, heads * HV),
            w_query.reshape(shard, 4, heads * FD),
            w_key.reshape(shard, 4, heads * FD),
        ],
        axis=2,
    )
    own_in = parts.astype(F32)
    w_in = (own_in * scale_one).astype(BF16)
    w_in = jnp.pad(w_in, ((0, 0), (0, 0), (0, 128 - 2 * heads * FD)))
    w_in = lax.all_gather(inward_rows(w_in), "g", axis=0, tiled=True)
    w_out = inward_cols(w_output.reshape(4, heads * HV, shard))
    w_out = lax.all_gather(w_out, "g", axis=1, tiled=True)

    own = (tokens[0].astype(F32) * mask).astype(BF16)
    all_tokens = gather_rows(own)

    scale_two = gain_two.astype(F32)[:, None, None]
    own_gate = w_gate.reshape(shard, 4, hidden_units).astype(F32)
    own_up = w_up.reshape(shard, 4, hidden_units).astype(F32)
    gate_w = inward_rows((own_gate * scale_two).astype(BF16))
    up_w = inward_rows((own_up * scale_two).astype(BF16))
    down_w = inward_cols(w_down.reshape(4, hidden_units, shard))
    gate_w = lax.all_gather(gate_w, "g", axis=0, tiled=True)
    up_w = lax.all_gather(up_w, "g", axis=0, tiled=True)
    down_w = lax.all_gather(down_w, "g", axis=1, tiled=True)

    size = 2 * local_rows
    part, proj, mixed, scale = attention(half_index, all_tokens, w_in, w_out, size)
    hidden = own.astype(F32) + scatter_rows(part)
    r_two = lax.rsqrt(jnp.mean(hidden * hidden, axis=-1, keepdims=True) + EPS)
    normed = gather_rows((hidden * r_two).astype(BF16))
    gate = dot(normed, gate_w, 1, 0)
    upward = dot(normed, up_w, 1, 0)
    sig = jax.nn.sigmoid(gate)
    silu = gate * sig
    activation = (silu * upward).astype(BF16)
    feed = scatter_rows(dot(activation, down_w, 1, 0).astype(BF16))
    result = ((hidden + feed) * mask).astype(BF16)[None]

    out_back = cotangent[0].astype(F32) * mask
    feed_back = gather_rows(out_back.astype(BF16))
    grad_down = dot(activation, feed_back, 0, 0).astype(BF16)
    act_back = dot(feed_back, down_w, 1, 1)
    up_back = (act_back * silu).astype(BF16)
    gate_back = (act_back * upward * sig * (1.0 + gate * (1.0 - sig))).astype(BF16)
    grad_gate = dot(normed, gate_back, 0, 0).astype(BF16)
    grad_up = dot(normed, up_back, 0, 0).astype(BF16)
    y_two = scatter_rows((dot(gate_back, gate_w, 1, 1) + dot(up_back, up_w, 1, 1)).astype(BF16))
    hidden_back = (
        out_back
        + r_two * y_two
        - hidden * (r_two**3 * jnp.mean(y_two * hidden, axis=-1, keepdims=True))
    )
    branch_back = gather_rows(hidden_back.astype(BF16))
    part, grad_in, grad_out = attention_back(
        half_index, branch_back, all_tokens, w_in, w_out, proj, mixed, scale, size
    )
    y_one = scatter_rows(part)
    wide = own.astype(F32)
    r_sq = 1.0 / (jnp.mean(wide * wide, axis=-1, keepdims=True) + EPS)
    masked_back = y_one - wide * (r_sq * jnp.mean(y_one * wide, axis=-1, keepdims=True))
    input_grad = ((hidden_back + masked_back) * mask).astype(BF16)[None]

    def rows_of(grad):
        return outward_rows(lax.psum_scatter(grad, "g", scatter_dimension=0, tiled=True)).astype(F32)

    def cols_of(grad):
        out = outward_cols(lax.psum_scatter(grad, "g", scatter_dimension=1, tiled=True))
        return out.reshape(-1, shard).astype(F32)

    grad_down = cols_of(grad_down)
    grad_gate = rows_of(grad_gate)
    grad_up = rows_of(grad_up)
    grad_out = cols_of(grad_out)
    grad_in = rows_of(grad_in)[:, :, : own_in.shape[2]]
    sum_one = jnp.sum(own_in * grad_in, axis=(1, 2))
    sum_two = jnp.sum(own_gate * grad_gate + own_up * grad_up, axis=(1, 2))
    sums = jnp.stack([sum_one, sum_two])
    sums = sums + lax.ppermute(sums, "t", SWAP)
    grad_in = grad_in * scale_one
    wide_v, wide_qk = heads * HV, heads * FD
    return (
        result,
        input_grad,
        grad_in[:, :, wide_v : wide_v + wide_qk].reshape(shard, -1),
        grad_in[:, :, wide_v + wide_qk :].reshape(shard, -1),
        grad_in[:, :, :wide_v].reshape(shard, -1),
        grad_out,
        sums[0],
        (grad_gate * scale_two).reshape(shard, -1),
        (grad_up * scale_two).reshape(shard, -1),
        grad_down,
        sums[1],
    )


def solution(mesh):
    groups = mesh.shape["dp"] // 4
    grid = Mesh(mesh.devices.reshape(groups, 2, 2, mesh.shape["tensor"]), ("g", "x", "c", "t"))
    dp = ("g", "x", "c")
    tokens, rows, cols, vector = P(dp, "t", None), P(dp, "t"), P("t", dp), P(dp)
    return jax.shard_map(
        per_device,
        mesh=grid,
        in_specs=(
            tokens, vector, rows, rows, rows, cols, vector, rows, rows, cols, vector, tokens,
        ),
        out_specs=(
            tokens, tokens, rows, rows, rows, cols, vector, rows, rows, cols, vector,
        ),
        check_vma=False,
    )
```

time: 1920 us -> 797 us (0.42)
  waiting for transfers between devices: 1390 us -> 364 us
  matrix products: 251 us -> 99.4 us
  blocking collectives: 150 us -> 0 us
  local copies, waits for them, and re-layouts: 43.9 us -> 128 us
  starting transfers between devices: 1.27 us -> 58.4 us
  Pallas kernels: 0 us -> 45.4 us
  other arithmetic: 34.2 us -> 76.2 us
  loops' own time: 30.6 us -> 0 us
    reduce_scatter x11 -> x5, waiting for transfers between devices: 992 us -> 0.05 us  [the longest x3 0.04 us: rows_of(): lax.psum_scatter(grad, 'g', scatter_dimension=0, tiled=True)]
    all_gather x9 -> x5, waiting for transfers between devices: 393 us -> 76.2 us  [the longest x1 38.8 us: per_device(): w_in = lax.all_gather(inward_rows(w_in), 'g', axis=0, tiled=True)]
    ppermute x0 -> x61, waiting for transfers between devices: none -> 288 us  [the longest x20 79.8 us: trade(): got = lax.ppermute(pick(array, split, 1 - me), axis_name, SWAP)]
    dot_general x57 -> x9, matrix products: 251 us -> 99.4 us  [dot(): lax.dot_general(left, right, (((left_dim,), (right_dim,)), ((), ())), pre...]
    all_gather x4 -> x0, blocking collectives: 83.7 us -> none  [the longest x1 23.1 us: gather_attention(): lax.all_gather(gain_one, 'dp', axis=0, tiled=True)]
    unnamed x1 -> x0, blocking collectives: 61.3 us -> none
    ppermute x0 -> x61, starting transfers between devices: none -> 56.5 us  [the longest x20 13.8 us: trade(): got = lax.ppermute(pick(array, split, 1 - me), axis_name, SWAP)]
    pallas_call x0 -> x2, Pallas kernels: none -> 45.4 us  [the longest x1 31.5 us: attention_back(): pl.pallas_call(backward_kernel, out_shape=(jax.ShapeDtypeStruct((total, w...]
  transfers between devices with their start and end apart: 20 -> 71, of which waited for: 16 -> 32; matrix products, arithmetic and copies ran while one was open for 8% -> 30% of each run, Pallas kernels for 0% -> 4%
where the time goes in v1:
time: 797 us; the launch traced here: 788 us
  waiting for transfers between devices  364 us (46%)
  local copies, waits for them, and re-layouts  128 us (16%)
  matrix products  99.4 us (12%)
  other arithmetic  76.2 us (10%)
  starting transfers between devices  58.4 us (7%)
  Pallas kernels  45.4 us (6%)
  between operations  16.4 us (2%)
    dot_general x9, matrix products, dot(): lax.dot_general(left, right, (((left_dim,), (right_dim,)), ((), ())), pre...  99.4 us
    ppermute x20, waiting for transfers between devices, trade(): got = lax.ppermute(pick(array, split, 1 - me), axis_name, SWAP)  79.8 us
    unnamed x150, local copies, waits for them, and re-layouts  49 us
    ppermute x4, waiting for transfers between devices, gather_rows(): from_x = lax.ppermute(block, 'x', SWAP)  47 us
    ppermute x4, waiting for transfers between devices, scatter_rows(): last_t = lax.ppermute(add(tops[1], got_x[half:]), 't', SWAP)  44 us
    ppermute x4, waiting for transfers between devices, scatter_rows(): got_x = lax.ppermute(jnp.concatenate([tops[2], tops[3]], axis=0), 'x', SWAP)  43.9 us
    all_gather x1, waiting for transfers between devices, per_device(): w_in = lax.all_gather(inward_rows(w_in), 'g', axis=0, tiled=True)  38.8 us
    pallas_call x1, Pallas kernels, attention_back(): pl.pallas_call(backward_kernel, out_shape=(jax.ShapeDtypeStruct((total, w...  31.5 us
  transfers between devices with their start and end apart: 71, of which 32 were waited for; matrix products, arithmetic and copies ran while one was open for 30% of the time, Pallas kernels for 4%

profile of v1, /device:TPU:0, one launch (start us, length us, event | category | flops | bytes accessed | tf_op | source)
XLA Modules:
  0.0 787.9 jit_solution(7701122216521396723)
XLA Ops:
  16.7 20.9 %collective-permute-done.1 = bf16[256,2048]{1,0:T(8,128)(2,1)S(1)} collective-permute-done((bf16[256,2048]{1,0:T(8,128)(2,1)S(1)}, bf16[256,2048]{1,0:T(8,128)(2,1)S(1)}, u32[]{:S(2)}, u32[]{:S(2)}) %collective-permute-start.1) | collective-permute-done | bytes 1048608 | tf_op jit(solution)/shard_map/ppermute | solution.py:24
  43.4 8.7 %collective-permute-done.2 = bf16[128,2048]{1,0:T(8,128)(2,1)S(1)} collective-permute-done((bf16[128,2048]{1,0:T(8,128)(2,1)S(1)}, bf16[128,2048]{1,0:T(8,128)(2,1)S(1)}, u32[]{:S(2)}, u32[]{:S(2)}) %collective-permute-start.2) | collective-permute-done | bytes 524320 | tf_op jit(solution)/shard_map/ppermute | solution.py:26
  80.1 12.7 %all-gather.8.cloned.1.call-done.wo_ref = bf16[256,2048]{1,0:T(8,128)(2,1)} async-done(((bf16[256,512]{1,0:T(8,128)(2,1)}), bf16[256,2048]{1,0:T(8,128)(2,1)}) %all-gather.8.cloned.1.call-update) | async-done | bytes 1048592 | tf_op jit(solution)/shard_map/all_gather | solution.py:320
  92.8 38.8 %all-gather.6.cloned.1.call-done.w_ref = bf16[2048,384]{1,0:T(8,128)(2,1)} async-done(((bf16[512,384]{1,0:T(8,128)(2,1)}), bf16[2048,384]{1,0:T(8,128)(2,1)}) %all-gather.6.cloned.1.call-update) | async-done | bytes 1572880 | tf_op jit(solution)/shard_map/all_gather | solution.py:318
  134.1 14.0 %shard_map.203 = (bf16[2048,2048]{1,0:T(8,128)(2,1)}, bf16[2048,384]{1,0:T(8,128)(2,1)S(1)}, bf16[2048,256]{1,0:T(8,128)(2,1)S(1)}, f32[2048,128]{1,0:T(8,128)S(1)}) custom-call(s32[1]{0:T(128)} %bitcast.1.half_ref, bf16[2048,2048]{1,0:T(8,128)(2,1)} %constant_dynamic-update-slice_fusion.5.u_ref, bf16[2048,384]{1,0:T(8,128)(2,1)S(1)} %copy-done, ...), custom_call_target="tpu_custom_call" | custom-call | flops 7516192768 | bytes 19922944 | tf_op jit(solution)/shard_map/pallas_call | solution.py:234
  164.1 9.2 %collective-permute-done.22 = bf16[2,128,704]{1,2,0:T(8,128)(2,1)S(1)} collective-permute-done((bf16[2,128,704]{1,2,0:T(8,128)(2,1)S(1)}, bf16[2,128,704]{1,2,0:T(8,128)(2,1)S(1)}, u32[]{:S(2)}, u32[]{:S(2)}) %collective-permute-start.22) | collective-permute-done | bytes 360480 | tf_op jit(solution)/shard_map/ppermute | solution.py:60
  187.4 21.5 %collective-permute-done.10 = bf16[256,2048]{1,0:T(8,128)(2,1)S(1)} collective-permute-done((bf16[256,2048]{1,0:T(8,128)(2,1)S(1)}, bf16[256,2048]{1,0:T(8,128)(2,1)S(1)}, u32[]{:S(2)}, u32[]{:S(2)}) %collective-permute-start.10) | collective-permute-done | bytes 1048608 | tf_op jit(solution)/shard_map/ppermute | solution.py:44
  212.9 11.0 %collective-permute-done.11 = bf16[128,2048]{1,0:T(8,128)(2,1)S(1)} collective-permute-done((bf16[128,2048]{1,0:T(8,128)(2,1)S(1)}, bf16[128,2048]{1,0:T(8,128)(2,1)S(1)}, u32[]{:S(2)}, u32[]{:S(2)}) %collective-permute-start.11) | collective-permute-done | bytes 524320 | tf_op jit(solution)/shard_map/ppermute | solution.py:46
  229.9 25.5 %collective-permute-done.20 = bf16[2,128,704]{1,2,0:T(8,128)(2,1)S(1)} collective-permute-done((bf16[2,128,704]{1,2,0:T(8,128)(2,1)S(1)}, bf16[2,128,704]{1,2,0:T(8,128)(2,1)S(1)}, u32[]{:S(2)}, u32[]{:S(2)}) %collective-permute-start.20) | collective-permute-done | bytes 360480 | tf_op jit(solution)/shard_map/ppermute | solution.py:60
  281.3 17.6 %collective-permute-done.15 = bf16[256,2048]{1,0:T(8,128)(2,1)S(1)} collective-permute-done((bf16[256,2048]{1,0:T(8,128)(2,1)S(1)}, bf16[256,2048]{1,0:T(8,128)(2,1)S(1)}, u32[]{:S(2)}, u32[]{:S(2)}) %collective-permute-start.15) | collective-permute-done | bytes 1048608 | tf_op jit(solution)/shard_map/ppermute | solution.py:24
  305.3 7.4 collective-permute-done.16
  324.0 9.2 %collective-permute-done.24 = bf16[704,2,128]{2,0,1:T(8,128)(2,1)S(1)} collective-permute-done((bf16[704,2,128]{2,0,1:T(8,128)(2,1)S(1)}, bf16[704,2,128]{2,0,1:T(8,128)(2,1)S(1)}, u32[]{:S(2)}, u32[]{:S(2)}) %collective-permute-start.24) | collective-permute-done | bytes 360480 | tf_op jit(solution)/shard_map/ppermute | solution.py:60
  348.3 11.0 %fusion.36 = f32[2048,704]{0,1:T(8,128)} fusion(bf16[2048,2048]{1,0:T(8,128)(2,1)} %constant_dynamic-update-slice_fusion.16, bf16[2048,704]{0,1:T(8,128)(2,1)} %all-gather.12.cloned.1.call-done), kind=kOutput, calls=%fused_computation.214 | convolution fusion | flops 5905580032 | bytes 17039360 | tf_op jit(solution)/shard_map/dot_general | solution.py:17
  359.3 11.1 %fusion.35 = f32[2048,704]{0,1:T(8,128)} fusion(bf16[2048,2048]{1,0:T(8,128)(2,1)} %constant_dynamic-update-slice_fusion.16, bf16[2048,704]{0,1:T(8,128)(2,1)} %all-gather.10.cloned.1.call-done), kind=kOutput, calls=%fused_computation.213 | convolution fusion | flops 5905580032 | bytes 17039360 | tf_op jit(solution)/shard_map/dot_general | solution.py:17
  370.4 24.8 %all-gather.14.cloned.1.call-done = bf16[704,2048]{1,0:T(8,128)(2,1)} async-done(((bf16[704,512]{1,0:T(8,128)(2,1)}), bf16[704,2048]{1,0:T(8,128)(2,1)}) %all-gather.14.cloned.1.call-update) | async-done | bytes 2883600 | tf_op jit(solution)/shard_map/all_gather | solution.py:333
  395.2 15.7 %multiply_convert_fusion = (bf16[2048,704]{0,1:T(8,128)(2,1)}, bf16[2048,704]{0,1:T(8,128)(2,1)S(1)}, bf16[2048,704]{0,1:T(8,128)(2,1)}) fusion(f32[2048,704]{0,1:T(8,128)} %fusion.35, f32[2048,704]{0,1:T(8,128)} %fusion.36, bf16[2048,2048]{1,0:T(8,128)(2,1)} %constant_dynamic-update-slice_fusion.27, bf16[704,2048]{1,0:T(8,128)(2,1)} %all-gather.14.cloned.1.call-done), kind=kOutput, calls=%fused_computation.6 | convolution fusion | flops 5927206912 | bytes 31457280 | tf_op jit(solution)/shard_map/dot_general | solution.py:17
  410.9 10.6 %fusion.37 = f32[2048,2048]{1,0:T(8,128)} fusion(bf16[2048,704]{0,1:T(8,128)(2,1)S(1)} %get-tuple-element.69, bf16[2048,704]{0,1:T(8,128)(2,1)S(1)} %copy-done.52), kind=kOutput, calls=%fused_computation.215 | convolution fusion | flops 5905580032 | bytes 22544384 | tf_op jit(solution)/shard_map/dot_general | solution.py:17
  421.5 11.2 %add_convert_fusion = bf16[2048,2048]{1,0:T(8,128)(2,1)S(1)} fusion(f32[2048,2048]{1,0:T(8,128)} %fusion.37, bf16[2048,704]{0,1:T(8,128)(2,1)} %get-tuple-element.68, bf16[2048,704]{0,1:T(8,128)(2,1)S(1)} %copy-done.51), kind=kOutput, calls=%fused_computation | convolution fusion | flops 5913968640 | bytes 30932992 | tf_op jit(solution)/shard_map/dot_general | solution.py:17
  437.8 10.9 %convolution_convert_fusion.3 = bf16[704,2048]{1,0:T(8,128)(2,1)} fusion(bf16[2048,704]{0,1:T(8,128)(2,1)S(1)} %copy-done.59, bf16[2048,2048]{1,0:T(8,128)(2,1)} %constant_dynamic-update-slice_fusion.27), kind=kOutput, calls=%fused_computation.13 | convolution fusion | flops 5907021824 | bytes 14155776 | tf_op jit(solution)/shard_map/dot_general | solution.py:17
  457.9 22.4 %collective-permute-done.36 = bf16[256,2048]{1,0:T(8,128)(2,1)S(1)} collective-permute-done((bf16[256,2048]{1,0:T(8,128)(2,1)S(1)}, bf16[256,2048]{1,0:T(8,128)(2,1)S(1)}, u32[]{:S(2)}, u32[]{:S(2)}) %collective-permute-start.36) | collective-permute-done | bytes 1048608 | tf_op jit(solution)/shard_map/ppermute | solution.py:44
  482.1 12.2 %collective-permute-done.37 = bf16[128,2048]{1,0:T(8,128)(2,1)S(1)} collective-permute-done((bf16[128,2048]{1,0:T(8,128)(2,1)S(1)}, bf16[128,2048]{1,0:T(8,128)(2,1)S(1)}, u32[]{:S(2)}, u32[]{:S(2)}) %collective-permute-start.37) | collective-permute-done | bytes 524320 | tf_op jit(solution)/shard_map/ppermute | solution.py:46
  497.3 11.0 %convolution_convert_fusion.2 = bf16[2048,704]{0,1:T(8,128)(2,1)} fusion(bf16[2048,704]{0,1:T(8,128)(2,1)S(1)} %copy-done.57, bf16[2048,2048]{1,0:T(8,128)(2,1)} %constant_dynamic-update-slice_fusion.16), kind=kOutput, calls=%fused_computation.12 | convolution fusion | flops 5907021824 | bytes 14155776 | tf_op jit(solution)/shard_map/dot_general | solution.py:17
  531.0 8.5 %collective-permute-done.41 = bf16[256,2048]{1,0:T(8,128)(2,1)S(1)} collective-permute-done((bf16[256,2048]{1,0:T(8,128)(2,1)S(1)}, bf16[256,2048]{1,0:T(8,128)(2,1)S(1)}, u32[]{:S(2)}, u32[]{:S(2)}) %collective-permute-start.41) | collective-permute-done | bytes 1048608 | tf_op jit(solution)/shard_map/ppermute | solution.py:24
  557.2 10.9 %convolution_convert_fusion.1 = bf16[2048,704]{0,1:T(8,128)(2,1)} fusion(bf16[2048,704]{0,1:T(8,128)(2,1)S(1)} %copy-done.58, bf16[2048,2048]{1,0:T(8,128)(2,1)} %constant_dynamic-update-slice_fusion.16), kind=kOutput, calls=%fused_computation.11 | convolution fusion | flops 5907021824 | bytes 14155776 | tf_op jit(solution)/shard_map/dot_general | solution.py:17
  582.7 31.5 %shard_map.204 = (bf16[2048,2048]{1,0:T(8,128)(2,1)}, bf16[2048,384]{1,0:T(8,128)(2,1)}, bf16[256,2048]{1,0:T(8,128)(2,1)}) custom-call(s32[1]{0:T(128)} %bitcast.1.half_ref, bf16[2048,2048]{1,0:T(8,128)(2,1)} %constant_dynamic-update-slice_fusion.38.back_ref, bf16[2048,2048]{1,0:T(8,128)(2,1)} %constant_dynamic-update-slice_fusion.5.u_ref, ...), custom_call_target="tpu_custom_call" | custom-call | flops 17179869184 | bytes 28311552 | tf_op jit(solution)/shard_map/pallas_call | solution.py:262
  635.8 10.8 %collective-permute-done.28 = bf16[256,2048]{1,0:T(8,128)(2,1)} collective-permute-done((bf16[256,2048]{1,0:T(8,128)(2,1)}, bf16[256,2048]{1,0:T(8,128)(2,1)}, u32[]{:S(2)}, u32[]{:S(2)}) %collective-permute-start.28) | collective-permute-done | bytes 1048608 | tf_op jit(solution)/shard_map/ppermute | solution.py:45
  647.4 9.9 %collective-permute-done.27 = bf16[128,2048]{1,0:T(8,128)(2,1)} collective-permute-done((bf16[128,2048]{1,0:T(8,128)(2,1)S(1)}, bf16[128,2048]{1,0:T(8,128)(2,1)}, u32[]{:S(2)}, u32[]{:S(2)}) %collective-permute-start.27) | collective-permute-done | bytes 524320 | tf_op jit(solution)/shard_map/ppermute | solution.py:46
  665.5 8.2 %collective-permute-done.29 = bf16[128,2048]{1,0:T(8,128)(2,1)S(1)} collective-permute-done((bf16[128,2048]{1,0:T(8,128)(2,1)S(1)}, bf16[128,2048]{1,0:T(8,128)(2,1)S(1)}, u32[]{:S(2)}, u32[]{:S(2)}) %collective-permute-start.29) | collective-permute-done | bytes 524320 | tf_op jit(solution)/shard_map/ppermute | solution.py:47
  701.1 15.8 %collective-permute-done.52 = bf16[256,2,128]{2,0,1:T(8,128)(2,1)} collective-permute-done((bf16[256,2,128]{2,0,1:T(8,128)(2,1)}, bf16[256,2,128]{2,0,1:T(8,128)(2,1)}, u32[]{:S(2)}, u32[]{:S(2)}) %collective-permute-start.52) | collective-permute-done | bytes 131104 | tf_op jit(solution)/shard_map/ppermute | solution.py:60
  726.9 19.3 %collective-permute-done.48 = bf16[256,2048]{1,0:T(8,128)(2,1)S(1)} collective-permute-done((bf16[256,2048]{1,0:T(8,128)(2,1)}, bf16[256,2048]{1,0:T(8,128)(2,1)S(1)}, u32[]{:S(2)}, u32[]{:S(2)}) %collective-permute-start.48) | collective-permute-done | bytes 1048608 | tf_op jit(solution)/shard_map/ppermute | solution.py:45
  746.3 11.0 %collective-permute-done.47 = bf16[128,2048]{1,0:T(8,128)(2,1)} collective-permute-done((bf16[128,2048]{1,0:T(8,128)(2,1)}, bf16[128,2048]{1,0:T(8,128)(2,1)}, u32[]{:S(2)}, u32[]{:S(2)}) %collective-permute-start.47) | collective-permute-done | bytes 524320 | tf_op jit(solution)/shard_map/ppermute | solution.py:46
  766.0 8.2 %collective-permute-done.49 = bf16[128,2048]{1,0:T(8,128)(2,1)} collective-permute-done((bf16[128,2048]{1,0:T(8,128)(2,1)}, bf16[128,2048]{1,0:T(8,128)(2,1)}, u32[]{:S(2)}, u32[]{:S(2)}) %collective-permute-start.49) | collective-permute-done | bytes 524320 | tf_op jit(solution)/shard_map/ppermute | solution.py:47
  (413 shorter events, 300.2 us)
Async XLA Ops:
  7.2 85.6 %all-gather.8.cloned.1.call-start = ((), (), s32[]{:S(2)}) async-start(), calls=%async_computation.6 | async-start | bytes 1310720 | tf_op jit(solution)/shard_map/all_gather | solution.py:320
  16.7 40.5 %collective-permute-start.7 = (bf16[2,256,128]{2,1,0:T(8,128)(2,1)}, bf16[2,256,128]{2,1,0:T(8,128)(2,1)S(1)}, u32[]{:S(2)}, u32[]{:S(2)}) collective-permute-start(bf16[2,256,128]{2,1,0:T(8,128)(2,1)} %get-tuple-element.175), channel_id=1, source_target_pairs={{0,2},{2,0},{1,3},{3,1},{4,6},{6,4},{5,7},{7,5},{8,10},{10,8},{9,1... | collective-permute-start | bytes 393224 | tf_op jit(solution)/shard_map/ppermute | solution.py:60
  64.4 67.1 %all-gather.6.cloned.1.call-start = ((), (), s32[]{:S(2)}) async-start(), calls=%async_computation.5 | async-start | bytes 1966080 | tf_op jit(solution)/shard_map/all_gather | solution.py:318
  75.2 273.0 %all-gather.12.cloned.1.call-start = ((), (), s32[]{:S(2)}) async-start(), calls=%async_computation.8 | async-start | bytes 3604480 | tf_op jit(solution)/shard_map/all_gather | solution.py:332
  178.1 181.2 %all-gather.10.cloned.1.call-start = ((), (), s32[]{:S(2)}) async-start(), calls=%async_computation.7 | async-start | bytes 3604480 | tf_op jit(solution)/shard_map/all_gather | solution.py:331
  185.8 27.1 %collective-permute-start.12 = (bf16[256,2048]{1,0:T(8,128)(2,1)S(1)}, bf16[256,2048]{1,0:T(8,128)(2,1)S(1)}, u32[]{:S(2)}, u32[]{:S(2)}) collective-permute-start(bf16[256,2048]{1,0:T(8,128)(2,1)S(1)} %pad_maximum_fusion.2), channel_id=1, source_target_pairs={{0,1},{1,0},{2,3},{3,2},{4,5},{5,4},{6,7},{7,6},{8,9},{9,8},{10,11... | collective-permute-start | bytes 3145736 | tf_op jit(solution)/shard_map/ppermute | solution.py:45
  210.7 49.6 %collective-permute-start.31 = (bf16[256,2048]{1,0:T(8,128)(2,1)}, bf16[256,2048]{1,0:T(8,128)(2,1)}, u32[]{:S(2)}, u32[]{:S(2)}) collective-permute-start(bf16[256,2048]{1,0:T(8,128)(2,1)} %get-tuple-element.63), channel_id=1, source_target_pairs={{0,4},{4,0},{1,5},{5,1},{2,6},{6,2},{3,7},{7,3},{8,12},{12,8},{9,1... | collective-permute-start | bytes 3145736 | tf_op jit(solution)/shard_map/ppermute | solution.py:24
  212.2 49.8 %collective-permute-start.30 = (bf16[256,2048]{1,0:T(8,128)(2,1)}, bf16[256,2048]{1,0:T(8,128)(2,1)}, u32[]{:S(2)}, u32[]{:S(2)}) collective-permute-start(bf16[256,2048]{1,0:T(8,128)(2,1)} %get-tuple-element.63), channel_id=1, source_target_pairs={{0,1},{1,0},{2,3},{3,2},{4,5},{5,4},{6,7},{7,6},{8,9},{9,8},{10,11... | collective-permute-start | bytes 3145736 | tf_op jit(solution)/shard_map/ppermute | solution.py:25
  225.5 39.1 %collective-permute-start.13 = (bf16[128,2048]{1,0:T(8,128)(2,1)}, bf16[128,2048]{1,0:T(8,128)(2,1)}, u32[]{:S(2)}, u32[]{:S(2)}) collective-permute-start(bf16[128,2048]{1,0:T(8,128)(2,1)} %get-tuple-element.90), channel_id=1, source_target_pairs={{0,4},{4,0},{1,5},{5,1},{2,6},{6,2},{3,7},{7,3},{8,12},{12,8},{9,1... | collective-permute-start | bytes 1572872 | tf_op jit(solution)/shard_map/ppermute | solution.py:47
  227.0 28.4 %collective-permute-start.20 = (bf16[2,128,704]{1,2,0:T(8,128)(2,1)S(1)}, bf16[2,128,704]{1,2,0:T(8,128)(2,1)S(1)}, u32[]{:S(2)}, u32[]{:S(2)}) collective-permute-start(bf16[2,128,704]{1,2,0:T(8,128)(2,1)S(1)} %get-tuple-element.133), channel_id=1, source_target_pairs={{0,4},{4,0},{1,5},{5,1},{2,6},{6,2},{3,7},{7,3},{8,12},{12,8},{9,1... | collective-permute-start | bytes 1081352 | tf_op jit(solution)/shard_map/ppermute | solution.py:60
  260.2 135.0 %all-gather.14.cloned.1.call-start = ((), (), s32[]{:S(2)}) async-start(), calls=%async_computation.9 | async-start | bytes 3604480 | tf_op jit(solution)/shard_map/all_gather | solution.py:333
  268.1 30.8 %collective-permute-start.15 = (bf16[256,2048]{1,0:T(8,128)(2,1)S(1)}, bf16[256,2048]{1,0:T(8,128)(2,1)S(1)}, u32[]{:S(2)}, u32[]{:S(2)}) collective-permute-start(bf16[256,2048]{1,0:T(8,128)(2,1)S(1)} %get-tuple-element.65), channel_id=1, source_target_pairs={{0,4},{4,0},{1,5},{5,1},{2,6},{6,2},{3,7},{7,3},{8,12},{12,8},{9,1... | collective-permute-start | bytes 3145736 | tf_op jit(solution)/shard_map/ppermute | solution.py:24
  268.6 31.8 %collective-permute-start.14 = (bf16[256,2048]{1,0:T(8,128)(2,1)S(1)}, bf16[256,2048]{1,0:T(8,128)(2,1)S(1)}, u32[]{:S(2)}, u32[]{:S(2)}) collective-permute-start(bf16[256,2048]{1,0:T(8,128)(2,1)S(1)} %get-tuple-element.65), channel_id=1, source_target_pairs={{0,1},{1,0},{2,3},{3,2},{4,5},{5,4},{6,7},{7,6},{8,9},{9,8},{10,11... | collective-permute-start | bytes 3145736 | tf_op jit(solution)/shard_map/ppermute | solution.py:25
  280.2 58.1 %collective-permute-start.34 = (bf16[1024,2048]{1,0:T(8,128)(2,1)}, bf16[1024,2048]{1,0:T(8,128)(2,1)}, u32[]{:S(2)}, u32[]{:S(2)}) collective-permute-start(bf16[1024,2048]{1,0:T(8,128)(2,1)} %get-tuple-element.146), channel_id=1, source_target_pairs={{0,2},{2,0},{1,3},{3,1},{4,6},{6,4},{5,7},{7,5},{8,10},{10,8},{9,1... | collective-permute-start | bytes 12582920 | tf_op jit(solution)/shard_map/ppermute | solution.py:29
  314.9 28.3 %collective-permute-start.18 = (bf16[1024,2048]{1,0:T(8,128)(2,1)}, bf16[1024,2048]{1,0:T(8,128)(2,1)}, u32[]{:S(2)}, u32[]{:S(2)}) collective-permute-start(bf16[1024,2048]{1,0:T(8,128)(2,1)} %get-tuple-element.150), channel_id=1, source_target_pairs={{0,2},{2,0},{1,3},{3,1},{4,6},{6,4},{5,7},{7,5},{8,10},{10,8},{9,1... | collective-permute-start | bytes 12582920 | tf_op jit(solution)/shard_map/ppermute | solution.py:29
  337.9 285.8 %reduce-scatter.14.cloned.1.call-start = ((), (), s32[]{:S(2)}) async-start(), calls=%async_computation.14 | async-start | bytes 3604480 | tf_op jit(solution)/shard_map/reduce_scatter | solution.py:376
  448.7 179.3 %reduce-scatter.10.cloned.1.call-start = ((), (), s32[]{:S(2)}) async-start(), calls=%async_computation.12 | async-start | bytes 3604480 | tf_op jit(solution)/shard_map/reduce_scatter | solution.py:373
  508.3 121.9 %reduce-scatter.12.cloned.1.call-start = ((), (), s32[]{:S(2)}) async-start(), calls=%async_computation.13 | async-start | bytes 3604480 | tf_op jit(solution)/shard_map/reduce_scatter | solution.py:373
  530.9 37.5 %collective-permute-start.25 = (bf16[1024,2048]{1,0:T(8,128)(2,1)}, bf16[1024,2048]{1,0:T(8,128)(2,1)}, u32[]{:S(2)}, u32[]{:S(2)}) collective-permute-start(bf16[1024,2048]{1,0:T(8,128)(2,1)} %slice.301), channel_id=1, source_target_pairs={{0,2},{2,0},{1,3},{3,1},{4,6},{6,4},{5,7},{7,5},{8,10},{10,8},{9,1... | collective-permute-start | bytes 12582920 | tf_op jit(solution)/shard_map/ppermute | solution.py:39
  568.1 111.2 %reduce-scatter.8.cloned.1.call-start = ((), (), s32[]{:S(2)}) async-start(), calls=%async_computation.11 | async-start | bytes 1310720 | tf_op jit(solution)/shard_map/reduce_scatter | solution.py:376
  576.5 44.5 %collective-permute-start.26 = (bf16[256,2048]{1,0:T(8,128)(2,1)}, bf16[256,2048]{1,0:T(8,128)(2,1)}, u32[]{:S(2)}, u32[]{:S(2)}) collective-permute-start(bf16[256,2048]{1,0:T(8,128)(2,1)} %pad_maximum_fusion.3), channel_id=1, source_target_pairs={{0,4},{4,0},{1,5},{5,1},{2,6},{6,2},{3,7},{7,3},{8,12},{12,8},{9,1... | collective-permute-start | bytes 3145736 | tf_op jit(solution)/shard_map/ppermute | solution.py:44
  619.0 62.0 %collective-permute-start.45 = (bf16[1024,2048]{1,0:T(8,128)(2,1)}, bf16[1024,2048]{1,0:T(8,128)(2,1)}, u32[]{:S(2)}, u32[]{:S(2)}) collective-permute-start(bf16[1024,2048]{1,0:T(8,128)(2,1)} %slice.264), channel_id=1, source_target_pairs={{0,2},{2,0},{1,3},{3,1},{4,6},{6,4},{5,7},{7,5},{8,10},{10,8},{9,1... | collective-permute-start | bytes 12582920 | tf_op jit(solution)/shard_map/ppermute | solution.py:39
  619.2 80.0 %reduce-scatter.6.cloned.1.call-start = ((), (), s32[]{:S(2)}) async-start(), calls=%async_computation.10 | async-start | bytes 1966080 | tf_op jit(solution)/shard_map/reduce_scatter | solution.py:373
  620.3 26.3 %collective-permute-start.28 = (bf16[256,2048]{1,0:T(8,128)(2,1)}, bf16[256,2048]{1,0:T(8,128)(2,1)}, u32[]{:S(2)}, u32[]{:S(2)}) collective-permute-start(bf16[256,2048]{1,0:T(8,128)(2,1)} %pad_maximum_fusion.4), channel_id=1, source_target_pairs={{0,1},{1,0},{2,3},{3,2},{4,5},{5,4},{6,7},{7,6},{8,9},{9,8},{10,11... | collective-permute-start | bytes 3145736 | tf_op jit(solution)/shard_map/ppermute | solution.py:45
  622.3 35.0 %collective-permute-start.27 = (bf16[128,2048]{1,0:T(8,128)(2,1)S(1)}, bf16[128,2048]{1,0:T(8,128)(2,1)}, u32[]{:S(2)}, u32[]{:S(2)}) collective-permute-start(bf16[128,2048]{1,0:T(8,128)(2,1)S(1)} %add_convert_fusion.10), channel_id=1, source_target_pairs={{0,1},{1,0},{2,3},{3,2},{4,5},{5,4},{6,7},{7,6},{8,9},{9,8},{10,11... | collective-permute-start | bytes 1572872 | tf_op jit(solution)/shard_map/ppermute | solution.py:46
  627.3 33.9 %collective-permute-start.59 = (bf16[704,2,128]{2,0,1:T(8,128)(2,1)}, bf16[704,2,128]{2,0,1:T(8,128)(2,1)}, u32[]{:S(2)}, u32[]{:S(2)}) collective-permute-start(bf16[704,2,128]{2,0,1:T(8,128)(2,1)} %bitcast.191), channel_id=1, source_target_pairs={{0,4},{4,0},{1,5},{5,1},{2,6},{6,2},{3,7},{7,3},{8,12},{12,8},{9,1... | collective-permute-start | bytes 1081352 | tf_op jit(solution)/shard_map/ppermute | solution.py:60
  634.5 28.7 %collective-permute-start.54 = (bf16[2,128,704]{1,2,0:T(8,128)(2,1)S(1)}, bf16[2,128,704]{1,2,0:T(8,128)(2,1)S(1)}, u32[]{:S(2)}, u32[]{:S(2)}) collective-permute-start(bf16[2,128,704]{1,2,0:T(8,128)(2,1)S(1)} %bitcast.223), channel_id=1, source_target_pairs={{0,4},{4,0},{1,5},{5,1},{2,6},{6,2},{3,7},{7,3},{8,12},{12,8},{9,1... | collective-permute-start | bytes 1081352 | tf_op jit(solution)/shard_map/ppermute | solution.py:60
  663.3 28.1 %collective-permute-start.60 = (bf16[2,704,128]{2,1,0:T(8,128)(2,1)}, bf16[2,704,128]{2,1,0:T(8,128)(2,1)}, u32[]{:S(2)}, u32[]{:S(2)}) collective-permute-start(bf16[2,704,128]{2,1,0:T(8,128)(2,1)} %get-tuple-element.114), channel_id=1, source_target_pairs={{0,2},{2,0},{1,3},{3,1},{4,6},{6,4},{5,7},{7,5},{8,10},{10,8},{9,1... | collective-permute-start | bytes 1081352 | tf_op jit(solution)/shard_map/ppermute | solution.py:60
  687.8 32.7 %collective-permute-start.46 = (bf16[256,2048]{1,0:T(8,128)(2,1)}, bf16[256,2048]{1,0:T(8,128)(2,1)}, u32[]{:S(2)}, u32[]{:S(2)}) collective-permute-start(bf16[256,2048]{1,0:T(8,128)(2,1)} %pad_maximum_fusion.7), channel_id=1, source_target_pairs={{0,4},{4,0},{1,5},{5,1},{2,6},{6,2},{3,7},{7,3},{8,12},{12,8},{9,1... | collective-permute-start | bytes 3145736 | tf_op jit(solution)/shard_map/ppermute | solution.py:44
  690.1 26.8 %collective-permute-start.52 = (bf16[256,2,128]{2,0,1:T(8,128)(2,1)}, bf16[256,2,128]{2,0,1:T(8,128)(2,1)}, u32[]{:S(2)}, u32[]{:S(2)}) collective-permute-start(bf16[256,2,128]{2,0,1:T(8,128)(2,1)} %bitcast.197), channel_id=1, source_target_pairs={{0,4},{4,0},{1,5},{5,1},{2,6},{6,2},{3,7},{7,3},{8,12},{12,8},{9,1... | collective-permute-start | bytes 393224 | tf_op jit(solution)/shard_map/ppermute | solution.py:60
  722.7 34.5 %collective-permute-start.47 = (bf16[128,2048]{1,0:T(8,128)(2,1)}, bf16[128,2048]{1,0:T(8,128)(2,1)}, u32[]{:S(2)}, u32[]{:S(2)}) collective-permute-start(bf16[128,2048]{1,0:T(8,128)(2,1)} %add_convert_fusion.6), channel_id=1, source_target_pairs={{0,1},{1,0},{2,3},{3,2},{4,5},{5,4},{6,7},{7,6},{8,9},{9,8},{10,11... | collective-permute-start | bytes 1572872 | tf_op jit(solution)/shard_map/ppermute | solution.py:46
  726.4 39.1 %collective-permute-start.58 = (f32[2,128]{1,0:T(2,128)S(1)}, f32[2,128]{1,0:T(2,128)S(1)}, u32[]{:S(2)}, u32[]{:S(2)}) collective-permute-start(f32[2,128]{1,0:T(2,128)S(1)} %pad_maximum_fusion.10), channel_id=1, source_target_pairs={{0,1},{1,0},{2,3},{3,2},{4,5},{5,4},{6,7},{7,6},{8,9},{9,8},{10,11... | collective-permute-start | bytes 3080 | tf_op jit(solution)/shard_map/ppermute | solution.py:387
  (100 other events, 1283.4 us)
Sparse Core Ops, SparseCore 0:
  64.5 28.2 all-gather.7
  94.9 36.5 all-gather.5
  178.2 57.9 all-gather.11
  260.3 57.0 all-gather.9
  338.0 57.0 all-gather.13
  448.8 55.0 reduce-scatter.13
  508.4 54.0 reduce-scatter.9
  568.2 54.1 reduce-scatter.11
  625.3 26.9 reduce-scatter.7
  664.1 33.0 reduce-scatter.5
